TPU v7x, 32 devices: a whole 2x2x4 slice. The times are simulated.
32 devices in a mesh: hid: 4 (over y, x), tok: 8 (over z, core).
Axes of the slice: x: 2, y: 2, z: 4, core: 2. Of those that a mesh axis runs over, the one named last changes fastest.
Arguments:
- keys: bfloat16 [2, 512, 1280], P(None, 'tok'), may hold values from -6 to 6
- values: bfloat16 [2, 512, 1280], P(None, 'tok'), may hold values from -6 to 6
- queries: bfloat16 [512, 1280], P('tok'), may hold values from -6 to 6
- rates: float32 [2, 512], P(None, 'tok'), may hold values from 0.01 to 0.1
- forget: float32 [2], replicated, may hold values from 0.05 to 0.3
- momentum: float32 [1], replicated, may hold values from 0.5 to 0.95
- write_weight: float32 [1280, 1280], P('tok', 'hid'), may hold values from -0.15625 to 0.15625
- read_weight: float32 [1280, 1280], P('tok', 'hid'), may hold values from -0.15625 to 0.15625
Outputs:
- new_write: float32 [1280, 1280], P('tok', 'hid')
- new_read: float32 [1280, 1280], P('tok', 'hid')
- recalled: bfloat16 [512, 1280], P('tok')
All inputs are finite; a program needn't handle non-finite values.
Results may differ from a plain program's by a relative error of at most 0.003.
Values may be sent and summed in bfloat16 or wider, within the bound.
No kernel may reach another device: no remote copies, remote signals or barrier semaphores. Data moves between devices by JAX's collectives and lax.ppermute only.
A program may use at most 64 MiB of HBM per device.

v0:
```python
import jax
import jax.numpy as jnp
from jax import lax
from jax.sharding import PartitionSpec as P

highest = lax.Precision.HIGHEST
radius = 12.0


def silu_slope(z):
    sig = jax.nn.sigmoid(z)
    return sig * (1.0 + z * (1.0 - sig))


def times_transposed(left, right):
    return lax.dot_general(left, right, (((1,), (1,)), ((), ())), precision=highest)


def inner_rows(left, right):
    return lax.dot_general(left, right, (((0,), (0,)), ((), ())), precision=highest)


def on_device(keys, values, queries, rates, forget, momentum, write_weight, read_weight):
    width = keys.shape[2]
    full_write, full_read = (
        lax.all_gather(write_weight, "tok", axis=0, tiled=True),
        lax.all_gather(read_weight, "tok", axis=0, tiled=True),
    )
    inputs = keys.reshape(-1, width).astype(jnp.float32)
    hidden_pre = jnp.dot(inputs, full_write, precision=highest)
    hidden = jax.nn.silu(hidden_pre)
    output = lax.psum(times_transposed(hidden, full_read).astype(jnp.bfloat16), "hid").astype(
        jnp.float32
    )
    error = inputs + output - values.reshape(-1, width).astype(jnp.float32)
    factor = 1.0 - forget[1] + momentum[0]
    per_block = jnp.stack([factor, jnp.ones_like(factor)])
    row_scale = (2.0 * rates * per_block[:, None]).reshape(-1, 1)
    delta = row_scale * error
    back = jnp.dot(delta, full_read, precision=highest) * silu_slope(hidden_pre)
    grad_write = inner_rows(inputs, back)
    grad_read = inner_rows(delta, hidden)
    part_w, part_r = (
        lax.psum_scatter(grad_write, "tok", scatter_dimension=0, tiled=True),
        lax.psum_scatter(grad_read, "tok", scatter_dimension=0, tiled=True),
    )
    keep = (1.0 - forget[0]) * (1.0 - forget[1])
    whole_w, whole_r = (
        lax.all_gather(part_w, "tok", axis=0, tiled=True),
        lax.all_gather(part_r, "tok", axis=0, tiled=True),
    )
    total = lax.psum(jnp.sum(whole_w * whole_w) + jnp.sum(whole_r * whole_r), "hid")
    scale = jnp.minimum(1.0, radius / jnp.sqrt(total + 1e-06))
    new_write = keep * write_weight - scale * part_w
    new_read = keep * read_weight - scale * part_r
    wide_write = keep * full_write - scale * whole_w
    wide_read = keep * full_read - scale * whole_r
    asked = queries.astype(jnp.float32)
    query_hidden = jax.nn.silu(jnp.dot(asked, wide_write, precision=highest))
    answer = lax.psum(times_transposed(query_hidden, wide_read), "hid")
    recalled = (asked + answer).astype(jnp.bfloat16)
    return (new_write, new_read, recalled)


def solution(mesh):
    in_specs = (
        P(None, "tok", None),
        P(None, "tok", None),
        P("tok", None),
        P(None, "tok"),
        P(),
        P(),
        P("tok", "hid"),
        P("tok", "hid"),
    )
    out_specs = (P("tok", "hid"), P("tok", "hid"), P("tok", None))
    return jax.shard_map(
        on_device, mesh=mesh, in_specs=in_specs, out_specs=out_specs, check_vma=False
    )
```

profile of v0, /device:TPU:0, one launch (start us, length us, event | category | flops | bytes accessed | tf_op | source)
XLA Modules:
  0.0 327.0 jit_solution(6038212173051882562)
XLA Ops:
  7.2 0.0 all-gather.5.cloned.1.call-start
  7.2 0.7 all-gather.5.cloned.1.call-update
  7.9 0.0 all-gather.7.cloned.1.call-start
  7.9 0.7 all-gather.7.cloned.1.call-update
  8.6 0.0 all-reduce.3.cloned.1.call-start
  9.3 1.3 fusion.33
  11.3 29.1 %all-gather.5.cloned.1.call-done = f32[1280,320]{1,0:T(8,128)} async-done(((f32[160,320]{1,0:T(8,128)}), f32[1280,320]{1,0:T(8,128)}) %all-gather.5.cloned.1.call-update) | async-done | bytes 1638416 | tf_op jit(solution)/shard_map/all_gather | solution.py:26
  40.4 3.4 %fusion.34 = f32[128,320]{0,1:T(8,128)S(1)} fusion(bf16[128,1280]{1,0:T(8,128)(2,1)} %bitcast.17, f32[1280,320]{1,0:T(8,128)} %all-gather.5.cloned.1.call-done), kind=kOutput, calls=%fused_computation.40 | convolution fusion | flops 629145600 | bytes 2129920 | tf_op jit(solution)/shard_map/dot_general | solution.py:30
  43.8 0.0 copy-start.10
  43.8 0.0 copy-start.2
  43.8 0.0 copy-start.3
  43.8 25.7 %all-gather.7.cloned.1.call-done = f32[1280,320]{1,0:T(8,128)} async-done(((f32[160,320]{1,0:T(8,128)}), f32[1280,320]{1,0:T(8,128)}) %all-gather.7.cloned.1.call-update) | async-done | bytes 1638416 | tf_op jit(solution)/shard_map/all_gather | solution.py:27
  69.6 4.6 %convolution_convert_fusion = bf16[128,1280]{1,0:T(8,128)(2,1)} fusion(f32[1280,320]{1,0:T(8,128)} %all-gather.7.cloned.1.call-done, f32[128,320]{0,1:T(8,128)S(1)} %fusion.34), kind=kOutput, calls=%fused_computation.1 | convolution fusion | flops 629473280 | bytes 2129920 | tf_op jit(solution)/shard_map/dot_general | solution.py:16
  74.2 0.0 all-reduce.3.cloned.1.call-update
  74.2 0.0 reduce-scatter.7.cloned.1.call-start
  74.3 0.1 maximum_multiply_fusion
  74.3 0.0 copy-done.10
  74.3 0.1 broadcast_multiply_fusion
  74.4 0.1 mul.101
  74.5 42.8 %all-reduce.3.cloned.1.call-done = bf16[128,1280]{1,0:T(8,128)(2,1)} async-done(((bf16[128,1280]{1,0:T(8,128)(2,1)}), bf16[128,1280]{1,0:T(8,128)(2,1)}) %all-reduce.3.cloned.1.call-update) | async-done | bytes 327696 | tf_op jit(solution)/shard_map/psum | solution.py:32
  117.3 0.0 copy-done.2
  117.4 0.0 copy-done.3
  117.4 0.0 copy-done
  117.4 4.3 %convolution_multiply_fusion = f32[128,320]{0,1:T(8,128)S(1)} fusion(f32[1280,320]{1,0:T(8,128)S(1)} %copy-done, bf16[128,1280]{1,0:T(8,128)(2,1)S(1)} %bitcast.21, bf16[128,1280]{1,0:T(8,128)(2,1)} %all-reduce.3.cloned.1.call-done, bf16[128,1280]{1,0:T(8,128)(2,1)S(1)} %bitcast.18, f32[128]{0:T(128)S(1)} %mul.101, f32[128,320]{0,1:T(8,128)S(1)} %fusion.34), kind=kOutput, calls=%fused_computation.12 | convolution fusion | flops 630456320 | bytes 2949632 | tf_op jit(solution)/shard_map/dot_general | solution.py:40
  121.6 2.0 convolution_bitcast_fusion
  123.6 2.8 copy.26
  126.4 0.0 reduce-scatter.7.cloned.1.call-update
  126.5 0.0 reduce-scatter.9.cloned.1.call-start
  126.5 0.0 copy-done.4
  126.5 3.7 %fusion.16 = f32[1280,320]{1,0:T(8,128)} fusion(bf16[128,1280]{1,0:T(8,128)(2,1)S(1)} %bitcast.22, bf16[128,1280]{1,0:T(8,128)(2,1)S(1)} %copy-done.4, bf16[128,1280]{1,0:T(8,128)(2,1)S(1)} %bitcast.20, f32[128]{0:T(128)S(1)} %mul.101, f32[128,320]{0,1:T(8,128)S(1)} %fusion.34), kind=kOutput, calls=%fused_computation.20 | convolution fusion | flops 630292480 | bytes 2785792
  130.2 0.0 reduce-scatter.9.cloned.1.call-update
  130.2 0.0 all-gather.9.cloned.1.call-start
  130.3 32.2 %reduce-scatter.7.cloned.1.call-done = f32[160,320]{1,0:T(8,128)} async-done(((f32[1280,320]{1,0:T(8,128)}), f32[160,320]{1,0:T(8,128)}) %reduce-scatter.7.cloned.1.call-update) | async-done | bytes 204816 | tf_op jit(solution)/shard_map/reduce_scatter | solution.py:44
  162.5 0.0 all-gather.9.cloned.1.call-update
  162.5 0.0 all-gather.11.cloned.1.call-start
  162.5 36.2 %reduce-scatter.9.cloned.1.call-done = f32[160,320]{1,0:T(8,128)} async-done(((f32[1280,320]{1,0:T(8,128)}), f32[160,320]{1,0:T(8,128)}) %reduce-scatter.9.cloned.1.call-update) | async-done | bytes 204816 | tf_op jit(solution)/shard_map/reduce_scatter | solution.py:45
  198.8 0.0 all-gather.11.cloned.1.call-update
  198.8 0.0 all-reduce.5.cloned.1.call-start
  199.5 0.0 copy-start.9
  199.5 27.1 %all-gather.9.cloned.1.call-done = f32[1280,320]{1,0:T(8,128)} async-done(((f32[160,320]{1,0:T(8,128)}), f32[1280,320]{1,0:T(8,128)}) %all-gather.9.cloned.1.call-update) | async-done | bytes 1638416 | tf_op jit(solution)/shard_map/all_gather | solution.py:49
  226.6 2.7 multiply_reduce_fusion.1
  229.3 26.5 %all-gather.11.cloned.1.call-done = f32[1280,320]{1,0:T(8,128)} async-done(((f32[160,320]{1,0:T(8,128)}), f32[1280,320]{1,0:T(8,128)}) %all-gather.11.cloned.1.call-update) | async-done | bytes 1638416 | tf_op jit(solution)/shard_map/all_gather | solution.py:50
  255.7 2.7 multiply_reduce_fusion
  259.7 10.5 %psum.22 = f32[]{:T(128)} all-reduce(f32[]{:T(128)S(6)} %add.42), channel_id=1, replica_groups=mesh['hid'=4,'tok'=8] {'hid'}, use_global_device_ids=true, to_apply=%region_5.6 | all-reduce | flops 1 | bytes 8 | tf_op jit(solution)/shard_map/psum | solution.py:52
  270.9 0.0 copy-done.9
  270.9 0.0 copy-start.1
  270.9 3.3 %fusion.8 = f32[64,320]{1,0:T(8,128)S(1)} fusion(bf16[64,1280]{1,0:T(8,128)(2,1)S(1)} %copy-done.9, f32[1280,320]{1,0:T(8,128)} %all-gather.9.cloned.1.call-done, f32[1280,320]{1,0:T(8,128)} %all-gather.5.cloned.1.call-done, f32[]{:T(128)S(6)} %min.3, f32[]{:T(128)} %bitcast), kind=kOutput, calls=%fused_computation.13 | convolution fusion | flops 315801600 | bytes 3522568 | tf_op jit(solution)/shard_map/dot_general | solution.py:59
  274.2 0.0 copy-done.1
  274.2 0.0 copy-start.5
  274.3 0.0 copy-start.6
  274.3 0.0 copy-start.7
  274.3 2.9 fusion
  277.2 0.0 all-reduce.5.cloned.1.call-update
  277.2 0.0 copy-done.5
  277.2 0.1 copy.18
  277.4 0.1 copy.22
  277.5 0.1 copy.27
  277.7 0.4 copy-done.8
  278.1 0.1 copy.29
  278.3 0.1 multiply_subtract_fusion
  278.4 0.8 copy.23
  279.2 0.8 copy.24
  280.0 38.5 %all-reduce.5.cloned.1.call-done = f32[64,1280]{1,0:T(8,128)} async-done(((f32[64,1280]{1,0:T(8,128)}), f32[64,1280]{1,0:T(8,128)}) %all-reduce.5.cloned.1.call-update) | async-done | bytes 327696 | tf_op jit(solution)/shard_map/psum | solution.py:60
  318.5 1.7 add_convert_fusion
  (5 shorter events, 0.0 us)
Async XLA Ops:
  7.2 33.3 %all-gather.5.cloned.1.call-start = ((), (), s32[]{:S(2)}) async-start(), calls=%async_computation.2 | async-start | bytes 2211840 | tf_op jit(solution)/shard_map/all_gather | solution.py:26
  7.9 61.7 %all-gather.7.cloned.1.call-start = ((), (), s32[]{:S(2)}) async-start(), calls=%async_computation.3 | async-start | bytes 2211840 | tf_op jit(solution)/shard_map/all_gather | solution.py:27
  8.6 108.7 %all-reduce.3.cloned.1.call-start = ((), (), s32[]{:S(2)}) async-start(), calls=%async_computation.4 | async-start | bytes 655360 | tf_op jit(solution)/shard_map/psum | solution.py:32
  43.8 30.5 %copy-start.10 = (f32[2,64]{1,0:T(2,128)S(1)}, f32[2,64]{1,0:T(2,128)}, u32[]{:S(2)}) copy-start(f32[2,64]{1,0:T(2,128)} %param.11) | copy-start | bytes 1540
  43.8 73.5 %copy-start.2 = (bf16[2,64,1280]{2,1,0:T(8,128)(2,1)S(1)}, bf16[2,64,1280]{2,1,0:T(8,128)(2,1)}, u32[]{:S(2)}) copy-start(bf16[2,64,1280]{2,1,0:T(8,128)(2,1)} %param.8) | copy-start | bytes 983044
  43.8 73.5 %copy-start.3 = (bf16[2,64,1280]{2,1,0:T(8,128)(2,1)S(1)}, bf16[2,64,1280]{2,1,0:T(8,128)(2,1)}, u32[]{:S(2)}) copy-start(bf16[2,64,1280]{2,1,0:T(8,128)(2,1)} %param.9) | copy-start | bytes 983044
  69.6 47.8 %copy-start = (f32[1280,320]{1,0:T(8,128)S(1)}, f32[1280,320]{1,0:T(8,128)}, u32[]{:S(2)}) copy-start(f32[1280,320]{1,0:T(8,128)} %all-gather.7.cloned.1.call-done) | copy-start | bytes 4915204
  74.2 88.2 %reduce-scatter.7.cloned.1.call-start = ((), (), s32[]{:S(2)}) async-start(), calls=%async_computation.8 | async-start | bytes 2211840 | tf_op jit(solution)/shard_map/reduce_scatter | solution.py:44
  123.6 2.9 copy-start.4
  126.5 72.3 %reduce-scatter.9.cloned.1.call-start = ((), (), s32[]{:S(2)}) async-start(), calls=%async_computation.9 | async-start | bytes 2211840 | tf_op jit(solution)/shard_map/reduce_scatter | solution.py:45
  130.2 96.4 %all-gather.9.cloned.1.call-start = ((), (), s32[]{:S(2)}) async-start(), calls=%async_computation.5 | async-start | bytes 2211840 | tf_op jit(solution)/shard_map/all_gather | solution.py:49
  162.5 93.3 %all-gather.11.cloned.1.call-start = ((), (), s32[]{:S(2)}) async-start(), calls=%async_computation.6 | async-start | bytes 2211840 | tf_op jit(solution)/shard_map/all_gather | solution.py:50
  198.8 119.7 %all-reduce.5.cloned.1.call-start = ((), (), s32[]{:S(2)}) async-start(), calls=%async_computation.7 | async-start | bytes 655360 | tf_op jit(solution)/shard_map/psum | solution.py:60
  199.5 71.5 %copy-start.9 = (bf16[64,1280]{1,0:T(8,128)(2,1)S(1)}, bf16[64,1280]{1,0:T(8,128)(2,1)}, u32[]{:S(2)}) copy-start(bf16[64,1280]{1,0:T(8,128)(2,1)} %param.10) | copy-start | bytes 491524
  270.9 3.3 %copy-start.1 = (f32[1280,320]{1,0:T(8,128)S(1)}, f32[1280,320]{1,0:T(8,128)}, u32[]{:S(2)}) copy-start(f32[1280,320]{1,0:T(8,128)} %all-gather.11.cloned.1.call-done) | copy-start | bytes 4915204
  274.2 2.9 copy-start.5
  274.3 3.1 copy-start.6
  274.3 3.2 copy-start.7
  277.2 0.9 copy-start.8
Sparse Core Ops, SparseCore 0:
  9.6 30.7 all-gather.4
  42.1 27.4 all-gather.6
  74.3 42.9 all-reduce.2
  126.6 35.8 reduce-scatter.6
  164.6 34.0 reduce-scatter.8
  200.2 26.3 all-gather.8
  228.2 27.4 all-gather.10
  277.3 41.1 all-reduce.4
where the time goes:
time: 327 us
  waiting for transfers between devices  260 us (80%)
  matrix products  24 us (7%)
  between operations  18.3 us (6%)
  blocking collectives  10.5 us (3%)
  other arithmetic  7.21 us (2%)
  local copies, waits for them, and re-layouts  6.97 us (2%)
    psum x1, waiting for transfers between devices, on_device(): lax.psum(times_transposed(hidden, full_read).astype(jnp.bfloat16), 'hid')  42.8 us
    psum x1, waiting for transfers between devices, on_device(): answer = lax.psum(times_transposed(query_hidden, wide_read), 'hid')  38.5 us
    reduce_scatter x1, waiting for transfers between devices, on_device(): lax.psum_scatter(grad_read, 'tok', scatter_dimension=0, tiled=True)  36.2 us
    reduce_scatter x1, waiting for transfers between devices, on_device(): lax.psum_scatter(grad_write, 'tok', scatter_dimension=0, tiled=True)  32.2 us
    all_gather x1, waiting for transfers between devices, on_device(): lax.all_gather(write_weight, 'tok', axis=0, tiled=True)  29.1 us
    all_gather x1, waiting for transfers between devices, on_device(): lax.all_gather(part_w, 'tok', axis=0, tiled=True)  27.1 us
    all_gather x1, waiting for transfers between devices, on_device(): lax.all_gather(part_r, 'tok', axis=0, tiled=True)  26.5 us
    all_gather x1, waiting for transfers between devices, on_device(): lax.all_gather(read_weight, 'tok', axis=0, tiled=True)  25.7 us
  transfers between devices with their start and end apart: 8, of which 8 were waited for; matrix products, arithmetic and copies ran while one was open for 4% of the time, Pallas kernels for 0%

commit v1 on v0

--- a/solution.py
+++ b/solution.py
@@ -29,9 +29,9 @@
     inputs = keys.reshape(-1, width).astype(jnp.float32)
     hidden_pre = jnp.dot(inputs, full_write, precision=highest)
     hidden = jax.nn.silu(hidden_pre)
-    output = lax.psum(times_transposed(hidden, full_read).astype(jnp.bfloat16), "hid").astype(
-        jnp.float32
-    )
+    output = jnp.sum(
+        lax.all_gather(times_transposed(hidden, full_read).astype(jnp.bfloat16), "hid"), axis=0
+    ).astype(jnp.float32)
     error = inputs + output - values.reshape(-1, width).astype(jnp.float32)
     factor = 1.0 - forget[1] + momentum[0]
     per_block = jnp.stack([factor, jnp.ones_like(factor)])

time: 327 us -> 313 us (0.957)
  waiting for transfers between devices: 260 us -> 245 us
    psum x1 -> x0, waiting for transfers between devices: 42.8 us -> none  [on_device(): lax.psum(times_transposed(hidden, full_read).astype(jnp.bfloat16), 'hid')]
    all_gather x0 -> x1, waiting for transfers between devices: none -> 26.1 us  [on_device(): lax.all_gather(times_transposed(hidden, full_read).astype(jnp.bfloat16),...]
where the time goes in v1:
time: 313 us
  waiting for transfers between devices  245 us (78%)
  matrix products  23.1 us (7%)
  between operations  18.3 us (6%)
  blocking collectives  10.5 us (3%)
  other arithmetic  8.74 us (3%)
  local copies, waits for them, and re-layouts  6.19 us (2%)
    psum x1, waiting for transfers between devices, on_device(): answer = lax.psum(times_transposed(query_hidden, wide_read), 'hid')  38.5 us
    reduce_scatter x1, waiting for transfers between devices, on_device(): lax.psum_scatter(grad_read, 'tok', scatter_dimension=0, tiled=True)  36.2 us
    reduce_scatter x1, waiting for transfers between devices, on_device(): lax.psum_scatter(grad_write, 'tok', scatter_dimension=0, tiled=True)  32.2 us
    all_gather x1, waiting for transfers between devices, on_device(): lax.all_gather(write_weight, 'tok', axis=0, tiled=True)  31.7 us
    all_gather x1, waiting for transfers between devices, on_device(): lax.all_gather(part_w, 'tok', axis=0, tiled=True)  27.1 us
    all_gather x1, waiting for transfers between devices, on_device(): lax.all_gather(part_r, 'tok', axis=0, tiled=True)  26.5 us
    all_gather x1, waiting for transfers between devices, on_device(): lax.all_gather(times_transposed(hidden, full_read).astype(jnp.bfloat16),...  26.1 us
    all_gather x1, waiting for transfers between devices, on_device(): lax.all_gather(read_weight, 'tok', axis=0, tiled=True)  25.7 us
  transfers between devices with their start and end apart: 8, of which 8 were waited for; matrix products, arithmetic and copies ran while one was open for 4% of the time, Pallas kernels for 0%

profile of v1, /device:TPU:0, one launch (start us, length us, event | category | flops | bytes accessed | tf_op | source)
XLA Modules:
  0.0 312.6 jit_solution(17086590941500771833)
XLA Ops:
  7.2 0.0 all-gather.7.cloned.1.call-start
  7.2 0.7 all-gather.7.cloned.1.call-update
  7.9 0.0 all-gather.9.cloned.1.call-start
  7.9 0.7 all-gather.9.cloned.1.call-update
  8.6 0.0 all-gather.15.cloned.1.call-start
  8.7 31.7 %all-gather.7.cloned.1.call-done = f32[1280,320]{1,0:T(8,128)} async-done(((f32[160,320]{1,0:T(8,128)}), f32[1280,320]{1,0:T(8,128)}) %all-gather.7.cloned.1.call-update) | async-done | bytes 1638416 | tf_op jit(solution)/shard_map/all_gather | solution.py:26
  40.4 3.4 %fusion.34 = f32[128,320]{0,1:T(8,128)S(1)} fusion(bf16[128,1280]{1,0:T(8,128)(2,1)} %bitcast.18, f32[1280,320]{1,0:T(8,128)} %all-gather.7.cloned.1.call-done), kind=kOutput, calls=%fused_computation.40 | convolution fusion | flops 629145600 | bytes 2129920 | tf_op jit(solution)/shard_map/dot_general | solution.py:30
  43.8 0.0 copy-start.9
  43.8 0.0 copy-start.10
  43.8 0.0 copy-start.2
  43.8 0.0 copy-start.3
  43.9 25.7 %all-gather.9.cloned.1.call-done = f32[1280,320]{1,0:T(8,128)} async-done(((f32[160,320]{1,0:T(8,128)}), f32[1280,320]{1,0:T(8,128)}) %all-gather.9.cloned.1.call-update) | async-done | bytes 1638416 | tf_op jit(solution)/shard_map/all_gather | solution.py:27
  69.6 4.6 %convolution_convert_fusion = bf16[128,1280]{1,0:T(8,128)(2,1)} fusion(f32[1280,320]{1,0:T(8,128)} %all-gather.9.cloned.1.call-done, f32[128,320]{0,1:T(8,128)S(1)} %fusion.34), kind=kOutput, calls=%fused_computation.1 | convolution fusion | flops 629473280 | bytes 2129920 | tf_op jit(solution)/shard_map/dot_general | solution.py:16
  74.2 0.0 all-gather.15.cloned.1.call-update
  74.2 0.0 reduce-scatter.7.cloned.1.call-start
  74.9 0.0 copy-done.9
  74.9 0.6 fusion.33
  76.2 0.1 maximum_multiply_fusion
  76.3 0.0 copy-done.10
  76.3 0.1 broadcast_multiply_fusion
  76.3 0.1 mul.101
  76.4 26.1 %all-gather.15.cloned.1.call-done = bf16[512,1280]{1,0:T(8,128)(2,1)} async-done(((bf16[128,1280]{1,0:T(8,128)(2,1)}), bf16[512,1280]{1,0:T(8,128)(2,1)}) %all-gather.15.cloned.1.call-update) | async-done | bytes 1310736 | tf_op jit(solution)/shard_map/all_gather | solution.py:33
  102.5 1.5 reduce_sum.30
  104.0 0.0 copy-done.2
  104.0 0.0 copy-done.3
  104.0 0.0 copy-done
  104.0 3.3 %convolution_multiply_fusion = f32[128,320]{0,1:T(8,128)S(1)} fusion(f32[1280,320]{1,0:T(8,128)S(1)} %copy-done, bf16[128,1280]{1,0:T(8,128)(2,1)S(1)} %bitcast.23, bf16[128,1280]{1,0:T(8,128)(2,1)S(1)} %reduce_sum.30, bf16[128,1280]{1,0:T(8,128)(2,1)S(1)} %bitcast.19, f32[128]{0:T(128)S(1)} %mul.101, f32[128,320]{0,1:T(8,128)S(1)} %fusion.34), kind=kOutput, calls=%fused_computation.12 | convolution fusion | flops 630456320 | bytes 2949632 | tf_op jit(solution)/shard_map/dot_general | solution.py:40
  107.3 2.0 convolution_bitcast_fusion
  109.3 2.8 copy.26
  112.1 0.0 reduce-scatter.7.cloned.1.call-update
  112.1 0.0 reduce-scatter.9.cloned.1.call-start
  112.2 3.7 %fusion.16 = f32[1280,320]{1,0:T(8,128)} fusion(bf16[128,1280]{1,0:T(8,128)(2,1)S(1)} %bitcast.24, bf16[128,1280]{1,0:T(8,128)(2,1)S(1)} %reduce_sum.30, bf16[128,1280]{1,0:T(8,128)(2,1)S(1)} %bitcast.21, f32[128]{0:T(128)S(1)} %mul.101, f32[128,320]{0,1:T(8,128)S(1)} %fusion.34), kind=kOutput, calls=%fused_computation.20 | convolution fusion | flops 630292480 | bytes 2785792
  115.8 0.0 reduce-scatter.9.cloned.1.call-update
  115.9 0.0 all-gather.11.cloned.1.call-start
  115.9 32.2 %reduce-scatter.7.cloned.1.call-done = f32[160,320]{1,0:T(8,128)} async-done(((f32[1280,320]{1,0:T(8,128)}), f32[160,320]{1,0:T(8,128)}) %reduce-scatter.7.cloned.1.call-update) | async-done | bytes 204816 | tf_op jit(solution)/shard_map/reduce_scatter | solution.py:44
  148.1 0.0 all-gather.11.cloned.1.call-update
  148.1 0.0 all-gather.13.cloned.1.call-start
  148.2 36.2 %reduce-scatter.9.cloned.1.call-done = f32[160,320]{1,0:T(8,128)} async-done(((f32[1280,320]{1,0:T(8,128)}), f32[160,320]{1,0:T(8,128)}) %reduce-scatter.9.cloned.1.call-update) | async-done | bytes 204816 | tf_op jit(solution)/shard_map/reduce_scatter | solution.py:45
  184.4 0.0 all-gather.13.cloned.1.call-update
  184.4 0.0 all-reduce.2.cloned.1.call-start
  185.1 0.0 copy-start.8
  185.1 27.1 %all-gather.11.cloned.1.call-done = f32[1280,320]{1,0:T(8,128)} async-done(((f32[160,320]{1,0:T(8,128)}), f32[1280,320]{1,0:T(8,128)}) %all-gather.11.cloned.1.call-update) | async-done | bytes 1638416 | tf_op jit(solution)/shard_map/all_gather | solution.py:49
  212.2 2.7 multiply_reduce_fusion.1
  214.8 26.5 %all-gather.13.cloned.1.call-done = f32[1280,320]{1,0:T(8,128)} async-done(((f32[160,320]{1,0:T(8,128)}), f32[1280,320]{1,0:T(8,128)}) %all-gather.13.cloned.1.call-update) | async-done | bytes 1638416 | tf_op jit(solution)/shard_map/all_gather | solution.py:50
  241.3 2.7 multiply_reduce_fusion
  245.3 10.5 %psum.14 = f32[]{:T(128)} all-reduce(f32[]{:T(128)S(6)} %add.40), channel_id=1, replica_groups=mesh['hid'=4,'tok'=8] {'hid'}, use_global_device_ids=true, to_apply=%region_5.6 | all-reduce | flops 1 | bytes 8 | tf_op jit(solution)/shard_map/psum | solution.py:52
  256.5 0.0 copy-done.8
  256.5 3.3 %fusion.8 = f32[64,320]{1,0:T(8,128)S(1)} fusion(bf16[64,1280]{1,0:T(8,128)(2,1)S(1)} %copy-done.8, f32[1280,320]{1,0:T(8,128)} %all-gather.11.cloned.1.call-done, f32[1280,320]{1,0:T(8,128)} %all-gather.7.cloned.1.call-done, f32[]{:T(128)S(6)} %min.3, f32[]{:T(128)} %bitcast), kind=kOutput, calls=%fused_computation.13 | convolution fusion | flops 315801600 | bytes 3522568 | tf_op jit(solution)/shard_map/dot_general | solution.py:59
  259.8 0.0 copy-done.1
  259.8 0.0 copy-start.4
  259.9 0.0 copy-start.5
  259.9 2.9 fusion
  262.8 0.0 all-reduce.2.cloned.1.call-update
  262.8 0.0 copy-done.4
  262.8 0.1 copy.18
  263.0 0.1 copy.22
  263.1 0.1 copy.27
  263.3 0.4 copy-done.7
  263.7 0.1 copy.29
  263.8 0.1 multiply_subtract_fusion
  263.9 0.8 copy.23
  264.8 0.8 copy.24
  265.6 38.5 %all-reduce.2.cloned.1.call-done = f32[64,1280]{1,0:T(8,128)} async-done(((f32[64,1280]{1,0:T(8,128)}), f32[64,1280]{1,0:T(8,128)}) %all-reduce.2.cloned.1.call-update) | async-done | bytes 327696 | tf_op jit(solution)/shard_map/psum | solution.py:60
  304.1 1.7 add_convert_fusion
  (6 shorter events, 0.0 us)
Async XLA Ops:
  7.2 33.3 %all-gather.7.cloned.1.call-start = ((), (), s32[]{:S(2)}) async-start(), calls=%async_computation.2 | async-start | bytes 2211840 | tf_op jit(solution)/shard_map/all_gather | solution.py:26
  7.9 61.7 %all-gather.9.cloned.1.call-start = ((), (), s32[]{:S(2)}) async-start(), calls=%async_computation.3 | async-start | bytes 2211840 | tf_op jit(solution)/shard_map/all_gather | solution.py:27
  8.6 93.8 %all-gather.15.cloned.1.call-start = ((), (), s32[]{:S(2)}) async-start(), calls=%async_computation.7 | async-start | bytes 1638400 | tf_op jit(solution)/shard_map/all_gather | solution.py:33
  43.8 31.1 %copy-start.9 = (f32[2]{0:T(128)S(1)}, f32[2]{0:T(128)}, u32[]{:S(2)}) copy-start(f32[2]{0:T(128)} %param.12) | copy-start | bytes 28
  43.8 32.4 %copy-start.10 = (f32[2,64]{1,0:T(2,128)S(1)}, f32[2,64]{1,0:T(2,128)}, u32[]{:S(2)}) copy-start(f32[2,64]{1,0:T(2,128)} %param.11) | copy-start | bytes 1540
  43.8 60.2 %copy-start.2 = (bf16[2,64,1280]{2,1,0:T(8,128)(2,1)S(1)}, bf16[2,64,1280]{2,1,0:T(8,128)(2,1)}, u32[]{:S(2)}) copy-start(bf16[2,64,1280]{2,1,0:T(8,128)(2,1)} %param.8) | copy-start | bytes 983044
  43.8 60.2 %copy-start.3 = (bf16[2,64,1280]{2,1,0:T(8,128)(2,1)S(1)}, bf16[2,64,1280]{2,1,0:T(8,128)(2,1)}, u32[]{:S(2)}) copy-start(bf16[2,64,1280]{2,1,0:T(8,128)(2,1)} %param.9) | copy-start | bytes 983044
  69.6 34.4 %copy-start = (f32[1280,320]{1,0:T(8,128)S(1)}, f32[1280,320]{1,0:T(8,128)}, u32[]{:S(2)}) copy-start(f32[1280,320]{1,0:T(8,128)} %all-gather.9.cloned.1.call-done) | copy-start | bytes 4915204
  74.2 73.9 %reduce-scatter.7.cloned.1.call-start = ((), (), s32[]{:S(2)}) async-start(), calls=%async_computation.8 | async-start | bytes 2211840 | tf_op jit(solution)/shard_map/reduce_scatter | solution.py:44
  112.1 72.3 %reduce-scatter.9.cloned.1.call-start = ((), (), s32[]{:S(2)}) async-start(), calls=%async_computation.9 | async-start | bytes 2211840 | tf_op jit(solution)/shard_map/reduce_scatter | solution.py:45
  115.9 96.3 %all-gather.11.cloned.1.call-start = ((), (), s32[]{:S(2)}) async-start(), calls=%async_computation.4 | async-start | bytes 2211840 | tf_op jit(solution)/shard_map/all_gather | solution.py:49
  148.1 93.2 %all-gather.13.cloned.1.call-start = ((), (), s32[]{:S(2)}) async-start(), calls=%async_computation.5 | async-start | bytes 2211840 | tf_op jit(solution)/shard_map/all_gather | solution.py:50
  184.4 119.7 %all-reduce.2.cloned.1.call-start = ((), (), s32[]{:S(2)}) async-start(), calls=%async_computation.6 | async-start | bytes 655360 | tf_op jit(solution)/shard_map/psum | solution.py:60
  185.1 71.4 %copy-start.8 = (bf16[64,1280]{1,0:T(8,128)(2,1)S(1)}, bf16[64,1280]{1,0:T(8,128)(2,1)}, u32[]{:S(2)}) copy-start(bf16[64,1280]{1,0:T(8,128)(2,1)} %param.10) | copy-start | bytes 491524
  256.5 3.3 %copy-start.1 = (f32[1280,320]{1,0:T(8,128)S(1)}, f32[1280,320]{1,0:T(8,128)}, u32[]{:S(2)}) copy-start(f32[1280,320]{1,0:T(8,128)} %all-gather.13.cloned.1.call-done) | copy-start | bytes 4915204
  259.8 2.9 copy-start.4
  259.9 3.1 copy-start.5
  259.9 3.2 %copy-start.6 = (f32[160,320]{1,0:T(8,128)S(1)}, f32[160,320]{1,0:T(8,128)}, u32[]{:S(2)}) copy-start(f32[160,320]{1,0:T(8,128)} %reduce-scatter.7.cloned.1.call-done) | copy-start | bytes 614404
  262.8 0.9 copy-start.7
Sparse Core Ops, SparseCore 0:
  9.6 30.7 all-gather.6
  42.1 27.4 all-gather.8
  74.4 28.0 all-gather.14
  112.3 35.7 reduce-scatter.6
  150.3 34.0 reduce-scatter.8
  185.9 26.2 all-gather.10
  213.8 27.4 all-gather.12
  262.9 41.1 all-reduce.1
